TPU v7x, 128 devices: a whole 4x4x4 slice. The times are simulated.
128 devices in a mesh: seq: 32 (over z_hi, y, x), ch: 4 (over z_lo, core).
Axes of the slice: x: 4, y: 4, z: 4 (z_hi: 2, z_lo: 2; z = z_hi * 2 + z_lo), core: 2. Of those that a mesh axis runs over, the one named last changes fastest.
Arguments:
- tokens: bfloat16 [262144, 512], P('seq', 'ch'), may hold values from -6 to 6
- gate: bfloat16 [262144, 512], P('seq', 'ch'), may hold values from -6 to 6
- cotangent: bfloat16 [262144, 512], P('seq', 'ch'), may hold values from -6 to 6
- w_first: bfloat16 [1024, 1024], replicated, may hold values from -0.1875 to 0.1875
- w_second: bfloat16 [256, 256], replicated, may hold values from -0.375 to 0.375
Outputs:
- mixed: bfloat16 [262144, 512], P('seq', 'ch')
- grad_tokens: bfloat16 [262144, 512], P('seq', 'ch')
- grad_gate: bfloat16 [262144, 512], P('seq', 'ch')
- grad_first: float32 [1024, 1024], replicated
- grad_second: float32 [256, 256], replicated
All inputs are finite; a program needn't handle non-finite values.
Results may differ from a plain program's by a relative error of at most 0.0058.
Values may be sent and summed in bfloat16 or wider, within the bound.
No kernel may reach another device: no remote copies, remote signals or barrier semaphores. Data moves between devices by JAX's collectives and lax.ppermute only.
A program may use at most 128 MiB of HBM per device.

v0:
```python
import jax
import jax.numpy as jnp
from jax import lax
from jax.sharding import PartitionSpec as P


def local(tokens, gate, cotangent, w_first, w_second):
    seq_count = lax.axis_size("seq")
    chan_count = lax.axis_size("ch")
    width = tokens.shape[1]
    block = w_first.shape[0]
    local_blocks = tokens.shape[0] // block
    all_blocks = local_blocks * seq_count
    x_blocks = tokens.reshape(local_blocks, block, width)
    gate_f = gate.reshape(local_blocks, block, width).astype(jnp.float32)
    cot_blocks = cotangent.reshape(local_blocks, block, width)
    first = jnp.einsum("jk,ikc->ijc", w_first, x_blocks, preferred_element_type=jnp.float32)
    sig = jax.nn.sigmoid(gate_f)
    act = gate_f * sig
    slope = sig * (1.0 + gate_f * (1.0 - sig))
    hidden = (first * act).astype(jnp.bfloat16)
    hidden_t = lax.all_to_all(hidden, "seq", split_axis=1, concat_axis=0, tiled=True)
    mixed_t = jnp.einsum(
        "il,ljc->ijc", w_second, hidden_t, preferred_element_type=jnp.float32
    ).astype(jnp.bfloat16)
    mixed = lax.all_to_all(mixed_t, "seq", split_axis=0, concat_axis=1, tiled=True)
    cot_t = lax.all_to_all(cot_blocks, "seq", split_axis=1, concat_axis=0, tiled=True)
    grad_hidden_t = jnp.einsum(
        "il,ijc->ljc", w_second, cot_t, preferred_element_type=jnp.float32
    ).astype(jnp.bfloat16)
    grad_hidden = lax.all_to_all(grad_hidden_t, "seq", split_axis=0, concat_axis=1, tiled=True)
    second_term = jnp.einsum("ijc,ljc->il", cot_t, hidden_t, preferred_element_type=jnp.float32)
    gh_float = grad_hidden.astype(jnp.float32)
    grad_first_act = (gh_float * act).astype(jnp.bfloat16)
    grad_gate = (gh_float * first * slope).astype(jnp.bfloat16)
    grad_tokens = jnp.einsum(
        "jk,ijc->ikc", w_first, grad_first_act, preferred_element_type=jnp.float32
    ).astype(jnp.bfloat16)
    first_term = jnp.einsum(
        "ijc,ikc->jk", grad_first_act, x_blocks, preferred_element_type=jnp.float32
    )
    first_sum, second_sum = lax.psum((first_term, second_term), ("seq", "ch"))
    total_width = width * chan_count
    grad_first = first_sum / jnp.sqrt(jnp.float32(all_blocks * total_width))
    grad_second = second_sum / jnp.sqrt(jnp.float32(block * total_width))
    rows = local_blocks * block
    return (
        mixed.reshape(rows, width),
        grad_tokens.reshape(rows, width),
        grad_gate.reshape(rows, width),
        grad_first,
        grad_second,
    )


def solution(mesh):
    return jax.shard_map(
        local,
        mesh=mesh,
        in_specs=(P("seq", "ch"), P("seq", "ch"), P("seq", "ch"), P(), P()),
        out_specs=(P("seq", "ch"), P("seq", "ch"), P("seq", "ch"), P(), P()),
        check_vma=False,
    )
```

profile of v0, /device:TPU:1, one launch (start us, length us, event | category | flops | bytes accessed | tf_op | source)
XLA Modules:
  0.0 332.1 jit_solution(3215558701580187851)
XLA Ops:
  7.2 0.0 copy-start
  7.2 3.1 copy.85
  10.3 0.0 copy-start.6
  10.3 39.3 %all_to_all.60 = bf16[8,1024,128]{2,0,1:T(8,128)(2,1)S(1)} all-to-all(bf16[8,1024,128]{2,0,1:T(8,128)(2,1)S(1)} %copy.85), channel_id=1, replica_groups=mesh['seq'=32,'ch'=4] {'seq'}, dimensions={1} | all-to-all | bytes 4194304 | tf_op jit(solution)/shard_map/all_to_all | solution.py:27
  49.6 0.0 copy-start.2
  49.6 1.4 copy-done.2
  51.0 0.0 copy-done.6
  51.0 0.7 fusion.14
  51.7 2.7 copy.89
  54.4 4.8 %all-to-all-start.3 = ((bf16[256,32,128]{2,1,0:T(8,128)(2,1)}), bf16[256,32,128]{2,1,0:T(8,128)(2,1)}, u32[]{:S(2)}, u32[]{:S(2)}) async-start(bf16[256,32,128]{2,1,0:T(8,128)(2,1)} %copy.89), calls=%async_computation.3 | async-start | bytes 4194304 | tf_op jit(solution)/shard_map/all_to_all | solution.py:31
  59.2 4.1 %copy.78 = f32[8,1024,128]{1,2,0:T(8,128)} copy(bf16[8,1024,128]{2,1,0:T(8,128)(2,1)} %bitcast.77) | data formatting | bytes 6291456 | tf_op jit(solution)/shard_map/convert_element_type | solution.py:15
  63.3 23.5 %all-to-all-done.3 = bf16[256,32,128]{2,1,0:T(8,128)(2,1)} async-done(((bf16[256,32,128]{2,1,0:T(8,128)(2,1)}), bf16[256,32,128]{2,1,0:T(8,128)(2,1)}, u32[]{:S(2)}, u32[]{:S(2)}) %all-to-all-start.3) | async-done | bytes 2097184 | tf_op jit(solution)/shard_map/all_to_all | solution.py:31
  86.8 2.1 convert_bitcast_fusion
  88.9 2.6 copy.90
  91.6 5.4 %copy.91 = f32[8,1024,128]{1,2,0:T(8,128)} copy(f32[8,1024,128]{2,1,0:T(8,128)} %bitcast.71) | data formatting | bytes 8388608 | tf_op jit(solution)/shard_map/convert_element_type | solution.py:33
  97.0 0.0 copy-done
  97.0 8.7 %fusion.2 = (bf16[8,1024,128]{1,2,0:T(8,128)(2,1)}, bf16[8,1024,128]{1,2,0:T(8,128)(2,1)}, bf16[8,1024,128]{1,2,0:T(8,128)(2,1)}) fusion(f32[8,1024,128]{1,2,0:T(8,128)} %copy.91, f32[8,1024,128]{1,2,0:T(8,128)} %copy.78, bf16[8,1024,128]{2,1,0:T(8,128)(2,1)S(1)} %bitcast.69, bf16[1024,1024]{1,0:T(8,128)(2,1)} %param.8), kind=kOutput, calls=%fused_computation.5 | convolution fusion | flops 2163212288 | bytes 18874368 | tf_op jit(solution)/shard_map/jk,ikc->ijc/dot_general | solution.py:17
  105.6 4.2 %copy.79 = bf16[8,1024,128]{2,0,1:T(8,128)(2,1)} copy(bf16[8,1024,128]{1,2,0:T(8,128)(2,1)} %get-tuple-element.33) | data formatting | bytes 4194304 | tf_op jit(solution)/shard_map/convert_element_type | solution.py:21
  109.8 4.8 %all-to-all-start = ((bf16[8,1024,128]{2,0,1:T(8,128)(2,1)}), bf16[8,1024,128]{2,0,1:T(8,128)(2,1)}, u32[]{:S(2)}, u32[]{:S(2)}) async-start(bf16[8,1024,128]{2,0,1:T(8,128)(2,1)} %copy.79), calls=%async_computation | async-start | bytes 4194304 | tf_op jit(solution)/shard_map/all_to_all | solution.py:22
  114.6 0.2 all-reduce.3.cloned.1.call-start
  114.8 6.0 %convolution_bitcast_fusion = f32[1024,1024]{1,0:T(8,128)} fusion(bf16[8,1024,128]{1,2,0:T(8,128)(2,1)} %get-tuple-element.34, bf16[8,1024,128]{2,1,0:T(8,128)(2,1)S(1)} %bitcast.70), kind=kOutput, calls=%fused_computation.9 | convolution fusion | flops 2147483648 | bytes 8388608 | tf_op jit(solution)/shard_map/ijc,ikc->jk/dot_general | solution.py:39
  120.8 19.4 %all-to-all-done = bf16[8,1024,128]{2,0,1:T(8,128)(2,1)} async-done(((bf16[8,1024,128]{2,0,1:T(8,128)(2,1)}), bf16[8,1024,128]{2,0,1:T(8,128)(2,1)}, u32[]{:S(2)}, u32[]{:S(2)}) %all-to-all-start) | async-done | bytes 2097184 | tf_op jit(solution)/shard_map/all_to_all | solution.py:22
  140.2 0.0 copy-start.3
  140.2 2.2 copy.81
  142.4 0.0 copy-start.4
  142.4 1.3 copy-done.4
  143.7 0.0 copy-done.3
  143.7 1.7 fusion.21
  145.4 0.0 copy-start.5
  145.4 0.0 all-reduce.3.cloned.1.call-update
  145.4 1.6 copy-done.5
  147.0 3.0 convert_bitcast_fusion.2
  150.0 4.6 %copy.83 = bf16[256,32,128]{2,1,0:T(8,128)(2,1)} copy(bf16[256,32,128]{0,2,1:T(8,128)(2,1)} %convert_bitcast_fusion.2) | data formatting | bytes 4194304 | tf_op jit(solution)/shard_map/convert_element_type | solution.py:25
  154.6 5.4 %all-to-all-start.1 = ((bf16[256,32,128]{2,1,0:T(8,128)(2,1)}), bf16[256,32,128]{2,1,0:T(8,128)(2,1)S(1)}, u32[]{:S(2)}, u32[]{:S(2)}) async-start(bf16[256,32,128]{2,1,0:T(8,128)(2,1)} %copy.83), calls=%async_computation.1 | async-start | bytes 4194304 | tf_op jit(solution)/shard_map/all_to_all | solution.py:26
  160.0 3.9 %copy.95 = bf16[8,1024,128]{2,1,0:T(8,128)(2,1)} copy(bf16[8,1024,128]{1,2,0:T(8,128)(2,1)} %get-tuple-element.32) | data formatting | bytes 4194304 | tf_op jit(solution)/shard_map/convert_element_type | solution.py:35
  163.9 6.0 %convert_bitcast_fusion.1 = bf16[8,1024,128]{1,2,0:T(8,128)(2,1)} fusion(bf16[8,1024,128]{1,2,0:T(8,128)(2,1)} %get-tuple-element.34, bf16[1024,1024]{1,0:T(8,128)(2,1)} %param.8), kind=kOutput, calls=%fused_computation.19 | convolution fusion | flops 2148532224 | bytes 6291456 | tf_op jit(solution)/shard_map/jk,ijc->ikc/dot_general | solution.py:36
  169.9 3.9 %copy.92 = bf16[8,1024,128]{2,1,0:T(8,128)(2,1)} copy(bf16[8,1024,128]{1,2,0:T(8,128)(2,1)} %convert_bitcast_fusion.1) | data formatting | bytes 4194304 | tf_op jit(solution)/shard_map/convert_element_type | solution.py:38
  173.8 15.1 %all-to-all-done.1 = bf16[256,32,128]{2,1,0:T(8,128)(2,1)S(1)} async-done(((bf16[256,32,128]{2,1,0:T(8,128)(2,1)}), bf16[256,32,128]{2,1,0:T(8,128)(2,1)S(1)}, u32[]{:S(2)}, u32[]{:S(2)}) %all-to-all-start.1) | async-done | bytes 2097184 | tf_op jit(solution)/shard_map/all_to_all | solution.py:26
  188.9 1.8 copy.84
  190.6 128.4 %all-reduce.3.cloned.1.call-done = (f32[1024,1024]{1,0:T(8,128)}, f32[256,256]{0,1:T(8,128)}) async-done(((f32[1024,1024]{1,0:T(8,128)}, f32[256,256]{0,1:T(8,128)}), (f32[1024,1024]{1,0:T(8,128)}, f32[256,256]{0,1:T(8,128)})) %all-reduce.3.cloned.1.call-update) | async-done | bytes 4456464 | tf_op jit(solution)/shard_map/psum | solution.py:42
  319.1 0.0 copy-start.7
  319.1 0.0 copy-start.1
  319.1 5.3 %broadcast_multiply_fusion = f32[1024,1024]{1,0:T(8,128)} fusion(f32[1024,1024]{1,0:T(8,128)} %get-tuple-element.30), kind=kLoop, calls=%fused_computation.18 | loop fusion | flops 1048576 | bytes 8388608 | tf_op jit(solution)/shard_map/div | solution.py:44
  324.3 0.0 copy-done.7
  324.4 0.8 copy.98
  325.2 0.0 copy-done.1
  (1 shorter events, 0.0 us)
Async XLA Ops:
  7.2 89.8 %copy-start = (bf16[8192,128]{1,0:T(8,128)(2,1)S(1)}, bf16[8192,128]{1,0:T(8,128)(2,1)}, u32[]{:S(2)}) copy-start(bf16[8192,128]{1,0:T(8,128)(2,1)} %param.5) | copy-start | bytes 6291460
  10.3 40.7 %copy-start.6 = (bf16[256,256]{1,0:T(8,128)(2,1)S(1)}, bf16[256,256]{1,0:T(8,128)(2,1)}, u32[]{:S(2)}) copy-start(bf16[256,256]{1,0:T(8,128)(2,1)} %param.9) | copy-start | bytes 393220
  49.6 1.4 copy-start.2
  54.4 32.4 %all-to-all-start.3 = ((bf16[256,32,128]{2,1,0:T(8,128)(2,1)}), bf16[256,32,128]{2,1,0:T(8,128)(2,1)}, u32[]{:S(2)}, u32[]{:S(2)}) async-start(bf16[256,32,128]{2,1,0:T(8,128)(2,1)} %copy.89), calls=%async_computation.3 | async-start | bytes 4194304 | tf_op jit(solution)/shard_map/all_to_all | solution.py:31
  109.8 30.4 %all-to-all-start = ((bf16[8,1024,128]{2,0,1:T(8,128)(2,1)}), bf16[8,1024,128]{2,0,1:T(8,128)(2,1)}, u32[]{:S(2)}, u32[]{:S(2)}) async-start(bf16[8,1024,128]{2,0,1:T(8,128)(2,1)} %copy.79), calls=%async_computation | async-start | bytes 4194304 | tf_op jit(solution)/shard_map/all_to_all | solution.py:22
  114.6 204.5 %all-reduce.3.cloned.1.call-start = ((), (), s32[]{:S(2)}) async-start(), calls=%async_computation.4 | async-start | bytes 8912896 | tf_op jit(solution)/shard_map/psum | solution.py:42
  140.2 3.5 %copy-start.3 = (bf16[8,1024,128]{2,0,1:T(8,128)(2,1)S(1)}, bf16[8,1024,128]{2,0,1:T(8,128)(2,1)}, u32[]{:S(2)}) copy-start(bf16[8,1024,128]{2,0,1:T(8,128)(2,1)} %copy-done.2) | copy-start | bytes 6291460
  142.4 1.3 copy-start.4
  145.4 1.6 copy-start.5
  154.6 34.3 %all-to-all-start.1 = ((bf16[256,32,128]{2,1,0:T(8,128)(2,1)}), bf16[256,32,128]{2,1,0:T(8,128)(2,1)S(1)}, u32[]{:S(2)}, u32[]{:S(2)}) async-start(bf16[256,32,128]{2,1,0:T(8,128)(2,1)} %copy.83), calls=%async_computation.1 | async-start | bytes 4194304 | tf_op jit(solution)/shard_map/all_to_all | solution.py:26
  319.1 5.3 %copy-start.7 = (f32[256,256]{0,1:T(8,128)S(1)}, f32[256,256]{0,1:T(8,128)}, u32[]{:S(2)}) copy-start(f32[256,256]{0,1:T(8,128)} %get-tuple-element.31) | copy-start | bytes 786436
  319.1 6.1 %copy-start.1 = (bf16[8192,128]{1,0:T(8,128)(2,1)S(1)}, bf16[8192,128]{1,0:T(8,128)(2,1)}, u32[]{:S(2)}) copy-start(bf16[8192,128]{1,0:T(8,128)(2,1)} %param.5) | copy-start | bytes 6291460
Sparse Core Ops, SparseCore 0:
  145.5 173.4 all-reduce.2
where the time goes:
time: 333 us; the launch traced here: 332 us
  waiting for transfers between devices  186 us (56%)
  local copies, waits for them, and re-layouts  43.6 us (13%)
  blocking collectives  39.3 us (12%)
  matrix products  26 us (8%)
  starting transfers between devices  15.2 us (5%)
  between operations  14.1 us (4%)
  other arithmetic  7.44 us (2%)
    psum x1, waiting for transfers between devices, local(): first_sum, second_sum = lax.psum((first_term, second_term), ('seq', 'ch'))  128 us
    all_to_all x1, blocking collectives, local(): lax.all_to_all(cot_blocks, 'seq', split_axis=1, concat_axis=0, tiled=True)  39.3 us
    all_to_all x1, waiting for transfers between devices, local(): lax.all_to_all(grad_hidden_t, 'seq', split_axis=0, concat_axis=1, tiled=T...  23.5 us
    all_to_all x1, waiting for transfers between devices, local(): lax.all_to_all(hidden, 'seq', split_axis=1, concat_axis=0, tiled=True)  19.4 us
    all_to_all x1, waiting for transfers between devices, local(): lax.all_to_all(mixed_t, 'seq', split_axis=0, concat_axis=1, tiled=True)  15.1 us
    dot_general x1, matrix products, local(): jnp.einsum('jk,ikc->ijc', w_first, x_blocks, preferred_element_type=jnp.f...  8.67 us
    convert_element_type x2, local copies, waits for them, and re-layouts, local(): gh_float = grad_hidden.astype(jnp.float32)  8.05 us
  transfers between devices with their start and end apart: 4, of which 4 were waited for; matrix products, arithmetic and copies ran while one was open for 10% of the time, Pallas kernels for 0%

commit v1 on v0

--- a/solution.py
+++ b/solution.py
@@ -39,7 +39,7 @@
     first_term = jnp.einsum(
         "ijc,ikc->jk", grad_first_act, x_blocks, preferred_element_type=jnp.float32
     )
-    first_sum, second_sum = lax.psum((first_term, second_term), ("seq", "ch"))
+    first_sum, second_sum = lax.psum(lax.psum((first_term, second_term), "seq"), "ch")
     total_width = width * chan_count
     grad_first = first_sum / jnp.sqrt(jnp.float32(all_blocks * total_width))
     grad_second = second_sum / jnp.sqrt(jnp.float32(block * total_width))

time: 333 us -> 639 us (1.92)
  waiting for transfers between devices: 186 us -> 491 us
    psum x1 -> x2, waiting for transfers between devices: 128 us -> 443 us  [the longest x1 345 us: local(): lax.psum((first_term, second_term), 'seq')]
    all_to_all x1, waiting for transfers between devices: 15.1 us -> 4.45 us  [local(): lax.all_to_all(mixed_t, 'seq', split_axis=0, concat_axis=1, tiled=True)]
  transfers between devices with their start and end apart: 4 -> 5, of which waited for: 4 -> 5; matrix products, arithmetic and copies ran while one was open for 10% -> 5% of each run, Pallas kernels for 0% -> 0%
where the time goes in v1:
time: 639 us; the launch traced here: 638 us
  waiting for transfers between devices  491 us (77%)
  local copies, waits for them, and re-layouts  43.6 us (7%)
  blocking collectives  39.3 us (6%)
  matrix products  26 us (4%)
  starting transfers between devices  17.3 us (3%)
  between operations  14.1 us (2%)
  other arithmetic  7.44 us (1%)
    psum x1, waiting for transfers between devices, local(): lax.psum((first_term, second_term), 'seq')  345 us
    psum x1, waiting for transfers between devices, local(): lax.psum(lax.psum((first_term, second_term), 'seq'), 'ch')  97.9 us
    all_to_all x1, blocking collectives, local(): lax.all_to_all(cot_blocks, 'seq', split_axis=1, concat_axis=0, tiled=True)  39.3 us
    all_to_all x1, waiting for transfers between devices, local(): lax.all_to_all(grad_hidden_t, 'seq', split_axis=0, concat_axis=1, tiled=T...  23.5 us
    all_to_all x1, waiting for transfers between devices, local(): lax.all_to_all(hidden, 'seq', split_axis=1, concat_axis=0, tiled=True)  19.4 us
  transfers between devices with their start and end apart: 5, of which 5 were waited for; matrix products, arithmetic and copies ran while one was open for 5% of the time, Pallas kernels for 0%

profile of v1, /device:TPU:1, one launch (start us, length us, event | category | flops | bytes accessed | tf_op | source)
XLA Modules:
  0.0 638.4 jit_solution(1461534168892707439)
XLA Ops:
  7.2 0.0 copy-start
  7.2 3.1 copy.85
  10.3 0.0 copy-start.6
  10.3 39.3 %all_to_all.60 = bf16[8,1024,128]{2,0,1:T(8,128)(2,1)S(1)} all-to-all(bf16[8,1024,128]{2,0,1:T(8,128)(2,1)S(1)} %copy.85), channel_id=1, replica_groups=mesh['seq'=32,'ch'=4] {'seq'}, dimensions={1} | all-to-all | bytes 4194304 | tf_op jit(solution)/shard_map/all_to_all | solution.py:27
  49.6 0.0 copy-start.2
  49.6 1.4 copy-done.2
  51.0 0.0 copy-done.6
  51.0 0.7 fusion.14
  51.7 2.7 copy.89
  54.4 4.8 all-to-all-start.3
  59.2 4.1 copy.78
  63.3 23.5 %all-to-all-done.3 = bf16[256,32,128]{2,1,0:T(8,128)(2,1)} async-done(((bf16[256,32,128]{2,1,0:T(8,128)(2,1)}), bf16[256,32,128]{2,1,0:T(8,128)(2,1)}, u32[]{:S(2)}, u32[]{:S(2)}) %all-to-all-start.3) | async-done | bytes 2097184 | tf_op jit(solution)/shard_map/all_to_all | solution.py:31
  86.8 2.1 convert_bitcast_fusion
  88.9 2.6 copy.90
  91.6 5.4 copy.91
  97.0 0.0 copy-done
  97.0 8.7 %fusion.2 = (bf16[8,1024,128]{1,2,0:T(8,128)(2,1)}, bf16[8,1024,128]{1,2,0:T(8,128)(2,1)}, bf16[8,1024,128]{1,2,0:T(8,128)(2,1)}) fusion(f32[8,1024,128]{1,2,0:T(8,128)} %copy.91, f32[8,1024,128]{1,2,0:T(8,128)} %copy.78, bf16[8,1024,128]{2,1,0:T(8,128)(2,1)S(1)} %bitcast.69, bf16[1024,1024]{1,0:T(8,128)(2,1)} %param.8), kind=kOutput, calls=%fused_computation.5 | convolution fusion | flops 2163212288 | bytes 18874368 | tf_op jit(solution)/shard_map/jk,ikc->ijc/dot_general | solution.py:17
  105.7 4.2 copy.79
  109.8 4.8 all-to-all-start
  114.6 0.2 all-reduce.5.cloned.1.call-start
  114.8 6.0 convolution_bitcast_fusion
  120.8 19.4 %all-to-all-done = bf16[8,1024,128]{2,0,1:T(8,128)(2,1)} async-done(((bf16[8,1024,128]{2,0,1:T(8,128)(2,1)}), bf16[8,1024,128]{2,0,1:T(8,128)(2,1)}, u32[]{:S(2)}, u32[]{:S(2)}) %all-to-all-start) | async-done | bytes 2097184 | tf_op jit(solution)/shard_map/all_to_all | solution.py:22
  140.2 0.0 copy-start.3
  140.2 2.2 copy.81
  142.4 0.0 copy-start.4
  142.4 1.3 copy-done.4
  143.7 0.0 copy-done.3
  143.7 1.7 fusion.21
  145.4 0.0 all-reduce.5.cloned.1.call-update
  145.4 0.0 all-reduce.7.cloned.1.call-start
  145.5 345.5 %all-reduce.5.cloned.1.call-done = (f32[1024,1024]{1,0:T(8,128)}, f32[256,256]{0,1:T(8,128)}) async-done(((f32[1024,1024]{1,0:T(8,128)}, f32[256,256]{0,1:T(8,128)}), (f32[1024,1024]{1,0:T(8,128)}, f32[256,256]{0,1:T(8,128)})) %all-reduce.5.cloned.1.call-update) | async-done | bytes 4456464 | tf_op jit(solution)/shard_map/psum | solution.py:42
  490.9 0.0 copy-start.5
  490.9 0.0 all-reduce.7.cloned.1.call-update
  490.9 1.6 copy-done.5
  492.5 3.0 convert_bitcast_fusion.2
  495.5 4.5 copy.83
  500.0 7.5 %all-to-all-start.1 = ((bf16[256,32,128]{2,1,0:T(8,128)(2,1)}), bf16[256,32,128]{2,1,0:T(8,128)(2,1)S(1)}, u32[]{:S(2)}, u32[]{:S(2)}) async-start(bf16[256,32,128]{2,1,0:T(8,128)(2,1)} %copy.83), calls=%async_computation.1 | async-start | bytes 4194304 | tf_op jit(solution)/shard_map/all_to_all | solution.py:26
  507.5 3.9 copy.95
  511.4 5.9 convert_bitcast_fusion.1
  517.3 3.9 copy.92
  521.2 4.5 all-to-all-done.1
  525.7 1.8 copy.84
  527.5 97.9 %all-reduce.7.cloned.1.call-done = (f32[1024,1024]{1,0:T(8,128)}, f32[256,256]{0,1:T(8,128)}) async-done(((f32[1024,1024]{1,0:T(8,128)}, f32[256,256]{0,1:T(8,128)}), (f32[1024,1024]{1,0:T(8,128)}, f32[256,256]{0,1:T(8,128)})) %all-reduce.7.cloned.1.call-update) | async-done | bytes 4456464 | tf_op jit(solution)/shard_map/psum | solution.py:42
  625.4 0.0 copy-start.7
  625.4 0.0 copy-start.1
  625.4 5.3 broadcast_multiply_fusion
  630.7 0.0 copy-done.7
  630.7 0.8 copy.98
  631.6 0.0 copy-done.1
  (1 shorter events, 0.0 us)
Async XLA Ops:
  7.2 89.8 %copy-start = (bf16[8192,128]{1,0:T(8,128)(2,1)S(1)}, bf16[8192,128]{1,0:T(8,128)(2,1)}, u32[]{:S(2)}) copy-start(bf16[8192,128]{1,0:T(8,128)(2,1)} %param.5) | copy-start | bytes 6291460
  10.3 40.7 %copy-start.6 = (bf16[256,256]{1,0:T(8,128)(2,1)S(1)}, bf16[256,256]{1,0:T(8,128)(2,1)}, u32[]{:S(2)}) copy-start(bf16[256,256]{1,0:T(8,128)(2,1)} %param.9) | copy-start | bytes 393220
  49.6 1.4 copy-start.2
  54.4 32.4 %all-to-all-start.3 = ((bf16[256,32,128]{2,1,0:T(8,128)(2,1)}), bf16[256,32,128]{2,1,0:T(8,128)(2,1)}, u32[]{:S(2)}, u32[]{:S(2)}) async-start(bf16[256,32,128]{2,1,0:T(8,128)(2,1)} %copy.89), calls=%async_computation.3 | async-start | bytes 4194304 | tf_op jit(solution)/shard_map/all_to_all | solution.py:31
  109.8 30.4 %all-to-all-start = ((bf16[8,1024,128]{2,0,1:T(8,128)(2,1)}), bf16[8,1024,128]{2,0,1:T(8,128)(2,1)}, u32[]{:S(2)}, u32[]{:S(2)}) async-start(bf16[8,1024,128]{2,0,1:T(8,128)(2,1)} %copy.79), calls=%async_computation | async-start | bytes 4194304 | tf_op jit(solution)/shard_map/all_to_all | solution.py:22
  114.6 376.3 %all-reduce.5.cloned.1.call-start = ((), (), s32[]{:S(2)}) async-start(), calls=%async_computation.4 | async-start | bytes 8912896 | tf_op jit(solution)/shard_map/psum | solution.py:42
  140.2 3.5 copy-start.3
  142.4 1.3 copy-start.4
  145.4 480.0 %all-reduce.7.cloned.1.call-start = ((), (), s32[]{:S(2)}) async-start(), calls=%async_computation.5 | async-start | bytes 8912896 | tf_op jit(solution)/shard_map/psum | solution.py:42
  490.9 1.6 copy-start.5
  500.0 25.7 %all-to-all-start.1 = ((bf16[256,32,128]{2,1,0:T(8,128)(2,1)}), bf16[256,32,128]{2,1,0:T(8,128)(2,1)S(1)}, u32[]{:S(2)}, u32[]{:S(2)}) async-start(bf16[256,32,128]{2,1,0:T(8,128)(2,1)} %copy.83), calls=%async_computation.1 | async-start | bytes 4194304 | tf_op jit(solution)/shard_map/all_to_all | solution.py:26
  625.4 5.3 copy-start.7
  625.4 6.1 copy-start.1
Sparse Core Ops, SparseCore 0:
  145.5 345.3 all-reduce.4
  493.5 131.8 all-reduce.6
